TPU v7x, 32 devices: a whole 2x2x4 slice. The times are simulated.
32 devices in a mesh: scen: 8 (over y, x, core), bldg: 4 (over z).
Axes of the slice: x: 2, y: 2, z: 4, core: 2. Of those that a mesh axis runs over, the one named last changes fastest.
Arguments:
- demand: float32 [128, 1024, 96], P('scen', 'bldg'), may hold values from -6 to 6
- tariff: float32 [128, 96], P('scen'), may hold values from 0 to 0.5
- feeder_price: float32 [128, 8, 96], P('scen'), may hold values from 0 to 0.5
- multiplier: float32 [128, 1024, 96], P('scen', 'bldg'), may hold values from -2 to 2
- previous_mean: float32 [128, 1024, 96], P('scen', 'bldg'), may hold values from 0 to 1
- inverse: float32 [1024, 96, 96], P('bldg'), as said below
- power_limit: float32 [1024, 96], P('bldg'), may hold values from 0.5 to 2
- weights: float32 [128], P('scen'), may hold values from 0.1 to 1
- tree_node: int32 [2, 128], P(None, 'scen'), may hold values from 0 to 15, as said below
- building_feeder: int32 [1024], P('bldg'), may hold values from 0 to 7, as said below
- feeder_limit: float32 [8, 96], replicated, may hold values from 25.6 to 128
Outputs:
- plan: float32 [128, 1024, 96], P('scen', 'bldg')
- new_multiplier: float32 [128, 1024, 96], P('scen', 'bldg')
- new_price: float32 [128, 8, 96], P('scen')
Inputs may be any that keep to these rules, and one draw needn't show every extreme that they name: `tree_node`: scenarios that share a third-section node share the second-section node; each third-section node holds 8 scenarios, each second-section node 16 scenarios. `building_feeder`: every feeder has exactly 128 buildings. `inverse`: symmetric with a positive diagonal.
All inputs are finite; a program needn't handle non-finite values.
Results may differ from a plain program's by a relative error of at most 0.0001.
Values sent between devices are 32-bit elements; how exact they have to be, the bound alone decides.
A program may use at most 128 MiB of HBM per device.

v0:
```python
import jax
import jax.numpy as jnp
from jax import lax
from jax.sharding import PartitionSpec as P

FEED = 128
PROX = 12


HIGHEST = lax.Precision.HIGHEST


def node_tables(nodes, fine_count):
    root = jnp.ones((1, nodes.shape[1]), jnp.float32)
    coarse = (nodes[0][None, :] == jnp.arange(8)[:, None]).astype(jnp.float32)
    fine_table = (nodes[1][None, :] == jnp.arange(fine_count)[:, None]).astype(jnp.float32)
    return [root, coarse, fine_table]


def section_sums(tables, scen_weight, shared_part, section_len):
    sums_list = []
    totals_list = []
    for level in range(3):
        weighted = tables[level] * scen_weight[None, :]
        block = shared_part[:, :, level * section_len : (level + 1) * section_len]
        sums_list.append(jnp.einsum("ns,sbt->nbt", weighted, block, precision=HIGHEST))
        totals_list.append(jnp.sum(weighted, axis=1))
    return (sums_list, totals_list)


def spread_means(tables, sums_list, totals_list):
    pieces = []
    for level in range(3):
        means = sums_list[level] / totals_list[level][:, None, None]
        pieces.append(jnp.einsum("ns,nbt->sbt", tables[level], means, precision=HIGHEST))
    return jnp.concatenate(pieces, axis=2)


def per_device(
    demand,
    tariff,
    feeder_price,
    multiplier,
    previous_mean,
    inverse,
    power_limit,
    weights,
    tree_node,
    building_feeder,
    feeder_limit,
):
    feeders = feeder_price.shape[1]
    slot_count = demand.shape[2]
    section_len = slot_count // 4
    member = (building_feeder[:, None] == jnp.arange(feeders)[None, :]).astype(jnp.float32)
    local_price = jnp.einsum("bf,sft->sbt", member, feeder_price, precision=HIGHEST)
    linear = tariff[:, None, :] + local_price - demand
    fixed_part = 0.5 * previous_mean - linear - multiplier
    ceiling = power_limit[None, :, :]
    iterate = jnp.clip(previous_mean, 0.0, ceiling)
    scaled_dual = jnp.zeros_like(iterate)
    for iteration in range(PROX):
        right_side = iterate - scaled_dual + fixed_part
        primal = jnp.einsum("btk,sbk->sbt", inverse, right_side, precision=HIGHEST)
        updated = jnp.clip(primal + scaled_dual, 0.0, ceiling)
        scaled_dual = scaled_dual + primal - updated
        iterate = updated
    shared_part = iterate[:, :, : 3 * section_len]
    fine_count = lax.axis_size("scen") * demand.shape[0] // 8
    tables = node_tables(tree_node, fine_count)
    sums_list, totals_list = section_sums(tables, weights, shared_part, section_len)
    summed = lax.psum(
        (sums_list[0], sums_list[1], sums_list[2], totals_list[0], totals_list[1], totals_list[2]),
        "scen",
    )
    early_mean = spread_means(tables, list(summed[:3]), list(summed[3:]))
    mean = jnp.concatenate([early_mean, iterate[:, :, 3 * section_len :]], axis=2)
    new_multiplier = multiplier + 0.5 * (iterate - mean)
    partial_load = jnp.einsum("bf,sbt->sft", member, iterate, precision=HIGHEST)
    feeder_load = lax.psum(partial_load, "bldg")
    new_price = jnp.maximum(0.0, feeder_price + (feeder_load - feeder_limit[None, :, :]) / FEED)
    return (iterate, new_multiplier, new_price)


def solution(mesh):
    in_specs = (
        P("scen", "bldg", None),
        P("scen", None),
        P("scen", None, None),
        P("scen", "bldg", None),
        P("scen", "bldg", None),
        P("bldg", None, None),
        P("bldg", None),
        P("scen"),
        P(None, "scen"),
        P("bldg"),
        P(),
    )
    out_specs = (P("scen", "bldg", None), P("scen", "bldg", None), P("scen", None, None))
    return jax.shard_map(
        per_device, mesh=mesh, in_specs=in_specs, out_specs=out_specs, check_vma=False
    )
```

profile of v0, /device:TPU:0, one launch (start us, length us, event | category | flops | bytes accessed | tf_op | source)
XLA Modules:
  0.0 478.1 jit_solution(2997713545076335994)
XLA Ops:
  7.3 11.7 %copy.15 = f32[256,96,96]{2,1,0:T(8,128)} copy(f32[256,96,96]{0,2,1:T(8,128)} %param.16) | data formatting | bytes 18874368 | tf_op args[5]
  19.0 3.6 minimum_add_fusion
  22.6 1.9 copy.14
  24.5 22.8 %fusion.52 = f32[256,16,96]{2,1,0:T(8,128)} fusion(f32[16,256,96]{2,0,1:T(8,128)} %copy.14, f32[256,96,96]{2,1,0:T(8,128)} %copy.15), kind=kOutput, calls=%fused_computation.96 | convolution fusion | flops 452984832 | bytes 12582912 | tf_op jit(solution)/shard_map/btk,sbk->sbt/dot_general | solution.py:64
  47.3 1.9 copy.16
  49.2 1.4 fusion.6
  50.7 2.9 copy.17
  53.6 22.8 %fusion.53 = f32[256,16,96]{2,1,0:T(8,128)} fusion(f32[16,256,96]{2,0,1:T(8,128)} %copy.17, f32[256,96,96]{2,1,0:T(8,128)} %copy.15), kind=kOutput, calls=%fused_computation.97 | convolution fusion | flops 452984832 | bytes 12582912 | tf_op jit(solution)/shard_map/btk,sbk->sbt/dot_general | solution.py:64
  76.4 2.8 copy.19
  79.2 3.0 subtract_add_fusion.9
  82.2 2.9 copy.20
  85.1 22.9 %fusion.54 = f32[256,16,96]{2,1,0:T(8,128)} fusion(f32[16,256,96]{2,0,1:T(8,128)} %copy.20, f32[256,96,96]{2,1,0:T(8,128)} %copy.15), kind=kOutput, calls=%fused_computation.98 | convolution fusion | flops 452984832 | bytes 12582912 | tf_op jit(solution)/shard_map/btk,sbk->sbt/dot_general | solution.py:64
  108.1 2.8 copy.22
  110.8 4.2 subtract_add_fusion.8
  115.1 2.9 copy.23
  118.0 22.8 %fusion.55 = f32[256,16,96]{2,1,0:T(8,128)} fusion(f32[16,256,96]{2,0,1:T(8,128)} %copy.23, f32[256,96,96]{2,1,0:T(8,128)} %copy.15), kind=kOutput, calls=%fused_computation.99 | convolution fusion | flops 452984832 | bytes 12582912 | tf_op jit(solution)/shard_map/btk,sbk->sbt/dot_general | solution.py:64
  140.8 2.9 copy.25
  143.7 3.0 subtract_add_fusion.7
  146.7 2.9 copy.26
  149.7 23.0 %fusion.56 = f32[256,16,96]{2,1,0:T(8,128)} fusion(f32[16,256,96]{2,0,1:T(8,128)} %copy.26, f32[256,96,96]{2,1,0:T(8,128)} %copy.15), kind=kOutput, calls=%fused_computation.100 | convolution fusion | flops 452984832 | bytes 12582912 | tf_op jit(solution)/shard_map/btk,sbk->sbt/dot_general | solution.py:64
  172.7 2.8 copy.28
  175.4 4.2 subtract_add_fusion.6
  179.7 2.9 copy.29
  182.6 22.8 %fusion.57 = f32[256,16,96]{2,1,0:T(8,128)} fusion(f32[16,256,96]{2,0,1:T(8,128)} %copy.29, f32[256,96,96]{2,1,0:T(8,128)} %copy.15), kind=kOutput, calls=%fused_computation.101 | convolution fusion | flops 452984832 | bytes 12582912 | tf_op jit(solution)/shard_map/btk,sbk->sbt/dot_general | solution.py:64
  205.4 2.9 copy.31
  208.3 3.0 subtract_add_fusion.5
  211.3 2.9 copy.32
  214.3 23.2 %fusion.58 = f32[256,16,96]{2,1,0:T(8,128)} fusion(f32[16,256,96]{2,0,1:T(8,128)} %copy.32, f32[256,96,96]{2,1,0:T(8,128)} %copy.15), kind=kOutput, calls=%fused_computation.102 | convolution fusion | flops 452984832 | bytes 12582912 | tf_op jit(solution)/shard_map/btk,sbk->sbt/dot_general | solution.py:64
  237.4 2.8 copy.34
  240.2 4.2 subtract_add_fusion.4
  244.5 2.9 copy.35
  247.4 22.8 %fusion.59 = f32[256,16,96]{2,1,0:T(8,128)} fusion(f32[16,256,96]{2,0,1:T(8,128)} %copy.35, f32[256,96,96]{2,1,0:T(8,128)} %copy.15), kind=kOutput, calls=%fused_computation.103 | convolution fusion | flops 452984832 | bytes 12582912 | tf_op jit(solution)/shard_map/btk,sbk->sbt/dot_general | solution.py:64
  270.2 2.9 copy.37
  273.1 3.0 subtract_add_fusion.3
  276.1 2.9 copy.38
  279.1 22.9 %fusion.60 = f32[256,16,96]{2,1,0:T(8,128)} fusion(f32[16,256,96]{2,0,1:T(8,128)} %copy.38, f32[256,96,96]{2,1,0:T(8,128)} %copy.15), kind=kOutput, calls=%fused_computation.104 | convolution fusion | flops 452984832 | bytes 12582912 | tf_op jit(solution)/shard_map/btk,sbk->sbt/dot_general | solution.py:64
  302.0 2.8 copy.40
  304.8 4.2 subtract_add_fusion.2
  309.0 2.9 copy.41
  311.9 22.8 %fusion.61 = f32[256,16,96]{2,1,0:T(8,128)} fusion(f32[16,256,96]{2,0,1:T(8,128)} %copy.41, f32[256,96,96]{2,1,0:T(8,128)} %copy.15), kind=kOutput, calls=%fused_computation.105 | convolution fusion | flops 452984832 | bytes 12582912 | tf_op jit(solution)/shard_map/btk,sbk->sbt/dot_general | solution.py:64
  334.7 2.8 copy.43
  337.5 3.0 subtract_add_fusion.1
  340.5 2.9 copy.44
  343.4 23.0 %fusion.62 = f32[256,16,96]{2,1,0:T(8,128)} fusion(f32[16,256,96]{2,0,1:T(8,128)} %copy.44, f32[256,96,96]{2,1,0:T(8,128)} %copy.15), kind=kOutput, calls=%fused_computation.106 | convolution fusion | flops 452984832 | bytes 12582912 | tf_op jit(solution)/shard_map/btk,sbk->sbt/dot_general | solution.py:64
  366.4 2.8 copy.46
  369.2 3.7 subtract_add_fusion
  372.9 2.9 copy.47
  375.8 22.8 %fusion.63 = f32[256,16,96]{2,1,0:T(8,128)} fusion(f32[16,256,96]{2,0,1:T(8,128)} %copy.47, f32[256,96,96]{2,1,0:T(8,128)} %copy.15), kind=kOutput, calls=%fused_computation.107 | convolution fusion | flops 452984832 | bytes 12582912 | tf_op jit(solution)/shard_map/btk,sbk->sbt/dot_general | solution.py:64
  398.6 3.0 copy.49
  401.7 3.1 fusion.3
  404.9 0.5 copy-done.11
  405.5 1.4 fusion.19
  406.9 1.1 fusion.21
  408.2 6.7 %fusion.23 = f32[1,256,24]{0,1,2:T(8,128)} fusion(f32[16,256,24]{1,2,0:T(8,128)S(1)} %get-tuple-element.17, f32[16]{0:T(128)S(1)} %copy-done.8), kind=kOutput, calls=%fused_computation.60 | convolution fusion | flops 1179648 | bytes 417856 | tf_op jit(solution)/shard_map/ns,sbt->nbt/dot_general | solution.py:26
  414.9 2.4 copy.53
  417.4 0.6 reduce_sum.29
  418.0 0.9 convolution_bitcast_fusion
  418.8 25.7 %all-reduce = (f32[16]{0:T(128)S(1)}, f32[8]{0:T(128)S(1)}, f32[1,256,24]{1,2,0:T(8,128)S(1)}, f32[]{:T(128)}) all-reduce(f32[16]{0:T(128)S(1)} %select_reduce_fusion, f32[8]{0:T(128)S(1)} %select_reduce_fusion.1, f32[1,256,24]{1,2,0:T(8,128)S(1)} %copy.53, f32[]{:T(128)} %reduce_sum.29), channel_id=1, replica_groups=mesh['scen'=8,'bldg'=4] {'scen'}, use_global_device_ids=true, to_apply=%region_8.9 | all-reduce | flops 6169 | bytes 49352 | tf_op jit(solution)/shard_map/psum | solution.py:72
  444.5 0.6 divide_bitcast_fusion
  445.2 19.8 %psum.55 = f32[16,8,96]{2,1,0:T(8,128)S(1)} all-reduce(f32[16,8,96]{2,1,0:T(8,128)S(1)} %convolution_bitcast_fusion), channel_id=1, replica_groups=mesh['scen'=8,'bldg'=4] {'bldg'}, use_global_device_ids=true, to_apply=%region_9.10 | all-reduce | flops 12288 | bytes 98304 | tf_op jit(solution)/shard_map/psum | solution.py:80
  465.0 0.6 add_maximum_fusion
  466.0 1.3 fusion.28
  467.6 1.5 fusion.25
  469.4 1.5 fusion.1
  (33 shorter events, 1.3 us)
Async XLA Ops:
  7.2 11.8 %copy-start.7 = (f32[16,96]{1,0:T(8,128)S(1)}, f32[16,96]{1,0:T(8,128)}, u32[]{:S(2)}) copy-start(f32[16,96]{1,0:T(8,128)} %param.12) | copy-start | bytes 18436
  7.2 11.8 %copy-start.6 = (f32[16,8,96]{2,1,0:T(8,128)S(1)}, f32[16,8,96]{2,1,0:T(8,128)}, u32[]{:S(2)}) copy-start(f32[16,8,96]{2,1,0:T(8,128)} %param.13) | copy-start | bytes 147460
  7.2 11.8 %copy-start.1 = (f32[256,96]{0,1:T(8,128)S(1)}, f32[256,96]{0,1:T(8,128)}, u32[]{:S(2)}) copy-start(f32[256,96]{0,1:T(8,128)} %param.17) | copy-start | bytes 294916
  7.2 11.8 %copy-start.10 = (s32[256]{0:T(256)S(1)}, s32[256]{0:T(256)}, u32[]{:S(2)}) copy-start(s32[256]{0:T(256)} %param.20) | copy-start | bytes 3076
  7.2 458.8 %all-reduce.4.cloned.1.call-start = ((), (), s32[]{:S(2)}) async-start(), calls=%async_computation | async-start | bytes 1179648 | tf_op jit(solution)/shard_map/psum | solution.py:72
  140.8 2.9 copy-start.2
  205.4 2.9 copy-start.3
  270.2 2.9 copy-start.4
  404.7 64.6 %copy-start = (f32[16,256,96]{1,2,0:T(8,128)}, f32[16,256,96]{1,2,0:T(8,128)S(1)}, u32[]{:S(2)}) copy-start(f32[16,256,96]{1,2,0:T(8,128)S(1)} %fusion.3) | copy-start | bytes 4718596
  404.8 0.7 copy-start.11
  404.8 0.7 copy-start.8
  417.3 47.7 %copy-start.9 = (f32[8,96]{1,0:T(8,128)S(1)}, f32[8,96]{1,0:T(8,128)}, u32[]{:S(2)}) copy-start(f32[8,96]{1,0:T(8,128)} %param.21) | copy-start | bytes 9220
  467.3 2.1 copy-start.5
Sparse Core Ops, SparseCore 0:
  408.1 57.8 all-reduce.3
where the time goes:
time: 487 us; the launch traced here: 478 us
  matrix products  291 us (60%)
  local copies, waits for them, and re-layouts  82.7 us (17%)
  blocking collectives  45.5 us (9%)
  other arithmetic  43.8 us (9%)
  between operations  14.7 us (3%)
    dot_general x12, matrix products, per_device(): primal = jnp.einsum('btk,sbk->sbt', inverse, right_side, precision=HIGHEST)  275 us
    add x11, other arithmetic, per_device(): right_side = iterate - scaled_dual + fixed_part  37.1 us
    add x12, local copies, waits for them, and re-layouts, per_device(): right_side = iterate - scaled_dual + fixed_part  34.2 us
    dot_general x12, local copies, waits for them, and re-layouts, per_device(): primal = jnp.einsum('btk,sbk->sbt', inverse, right_side, precision=HIGHEST)  33.1 us
    psum x1, blocking collectives, per_device(): lax.psum((sums_list[0], sums_list[1], sums_list[2], totals_list[0], total...  25.7 us
    psum x1, blocking collectives, per_device(): feeder_load = lax.psum(partial_load, 'bldg')  19.8 us
    unnamed x25, local copies, waits for them, and re-layouts  12.3 us
  transfers between devices with their start and end apart: 1, of which 1 were waited for; matrix products, arithmetic and copies ran while one was open for 3% of the time, Pallas kernels for 0%

commit v1 on v0

--- a/solution.py
+++ b/solution.py
@@ -1,6 +1,8 @@
 import jax
 import jax.numpy as jnp
 from jax import lax
+from jax.experimental import pallas as pl
+from jax.experimental.pallas import tpu as pltpu
 from jax.sharding import PartitionSpec as P
 
 FEED = 128
@@ -36,6 +38,89 @@
     return jnp.concatenate(pieces, axis=2)
 
 
+BLOCK = 16
+LANES = 128
+
+
+def prox_kernel(
+    demand_ref, tariff_ref, price_ref, mult_ref, prev_ref, inv_ref, limit_ref, feeder_ref,
+    plan_ref, load_ref, w_ref, fixed_ref, z_ref, u_ref, price_t_ref,
+):
+    step = pl.program_id(0)
+    scen, block, slots = demand_ref.shape
+
+    @pl.when(step == 0)
+    def _():
+        load_ref[...] = jnp.zeros_like(load_ref)
+        price_t_ref[...] = tariff_ref[...][None] + jnp.transpose(price_ref[...], (1, 0, 2))
+
+    prev = jnp.transpose(prev_ref[...], (1, 0, 2))
+    rest = 0.5 * prev_ref[...] + demand_ref[...] - mult_ref[...]
+    fixed_ref[...] = jnp.transpose(rest, (1, 0, 2))
+    ceiling = limit_ref[...][:, None, :]
+    z_ref[...] = jnp.clip(prev, 0.0, ceiling)
+    u_ref[...] = jnp.zeros_like(u_ref)
+    for b in range(block):
+        fixed_ref[b] = fixed_ref[b] - price_t_ref[feeder_ref[step * block + b]]
+        full = inv_ref[b]
+        high = full.astype(jnp.bfloat16)
+        w_ref[b, :, :slots] = high
+        w_ref[b, :, LANES : LANES + slots] = (full - high.astype(jnp.float32)).astype(jnp.bfloat16)
+
+    def iteration(i, carry):
+        for b in range(block):
+            z, u = z_ref[b], u_ref[b]
+            right = z - u + fixed_ref[b]
+            high = right.astype(jnp.bfloat16)
+            low = (right - high.astype(jnp.float32)).astype(jnp.bfloat16)
+            both = jnp.concatenate([high, low], axis=0)
+            out = jnp.dot(both, w_ref[b], preferred_element_type=jnp.float32)
+            primal = out[:scen, :slots] + (out[:scen, LANES : LANES + slots] + out[scen:, :slots])
+            moved = primal + u
+            fresh = jnp.clip(moved, 0.0, limit_ref[b : b + 1, :])
+            z_ref[b] = fresh
+            u_ref[b] = moved - fresh
+        return carry
+
+    lax.fori_loop(0, PROX, iteration, 0)
+    for b in range(block):
+        load_ref[feeder_ref[step * block + b]] += z_ref[b]
+    plan_ref[...] = jnp.transpose(z_ref[...], (1, 0, 2))
+
+
+def prox(demand, tariff, feeder_price, multiplier, previous_mean, inverse, power_limit, building_feeder):
+    scen, count, slots = demand.shape
+    feeders = feeder_price.shape[1]
+    block = min(BLOCK, count)
+    big = pl.BlockSpec((scen, block, slots), lambda i: (0, i, 0))
+    whole2 = pl.BlockSpec((scen, slots), lambda i: (0, 0))
+    whole3 = pl.BlockSpec((scen, feeders, slots), lambda i: (0, 0, 0))
+    return pl.pallas_call(
+        prox_kernel,
+        grid=(count // block,),
+        in_specs=[
+            big, whole2, whole3, big, big,
+            pl.BlockSpec((block, slots, slots), lambda i: (i, 0, 0)),
+            pl.BlockSpec((block, slots), lambda i: (i, 0)),
+            pl.BlockSpec(memory_space=pltpu.SMEM),
+        ],
+        out_specs=[big, pl.BlockSpec((feeders, scen, slots), lambda i: (0, 0, 0))],
+        out_shape=[
+            jax.ShapeDtypeStruct((scen, count, slots), jnp.float32),
+            jax.ShapeDtypeStruct((feeders, scen, slots), jnp.float32),
+        ],
+        scratch_shapes=[
+            pltpu.VMEM((block, slots, 2 * LANES), jnp.bfloat16),
+            pltpu.VMEM((block, scen, slots), jnp.float32),
+            pltpu.VMEM((block, scen, slots), jnp.float32),
+            pltpu.VMEM((block, scen, slots), jnp.float32),
+            pltpu.VMEM((feeders, scen, slots), jnp.float32),
+        ],
+        compiler_params=pltpu.CompilerParams(dimension_semantics=("arbitrary",), vmem_limit_bytes=40 * 2**20),
+        name="prox",
+    )(demand, tariff, feeder_price, multiplier, previous_mean, inverse, power_limit, building_feeder)
+
+
 def per_device(
     demand,
     tariff,
@@ -49,22 +134,11 @@
     building_feeder,
     feeder_limit,
 ):
-    feeders = feeder_price.shape[1]
     slot_count = demand.shape[2]
     section_len = slot_count // 4
-    member = (building_feeder[:, None] == jnp.arange(feeders)[None, :]).astype(jnp.float32)
-    local_price = jnp.einsum("bf,sft->sbt", member, feeder_price, precision=HIGHEST)
-    linear = tariff[:, None, :] + local_price - demand
-    fixed_part = 0.5 * previous_mean - linear - multiplier
-    ceiling = power_limit[None, :, :]
-    iterate = jnp.clip(previous_mean, 0.0, ceiling)
-    scaled_dual = jnp.zeros_like(iterate)
-    for iteration in range(PROX):
-        right_side = iterate - scaled_dual + fixed_part
-        primal = jnp.einsum("btk,sbk->sbt", inverse, right_side, precision=HIGHEST)
-        updated = jnp.clip(primal + scaled_dual, 0.0, ceiling)
-        scaled_dual = scaled_dual + primal - updated
-        iterate = updated
+    iterate, partial_load = prox(
+        demand, tariff, feeder_price, multiplier, previous_mean, inverse, power_limit, building_feeder
+    )
     shared_part = iterate[:, :, : 3 * section_len]
     fine_count = lax.axis_size("scen") * demand.shape[0] // 8
     tables = node_tables(tree_node, fine_count)
@@ -76,8 +150,7 @@
     early_mean = spread_means(tables, list(summed[:3]), list(summed[3:]))
     mean = jnp.concatenate([early_mean, iterate[:, :, 3 * section_len :]], axis=2)
     new_multiplier = multiplier + 0.5 * (iterate - mean)
-    partial_load = jnp.einsum("bf,sbt->sft", member, iterate, precision=HIGHEST)
-    feeder_load = lax.psum(partial_load, "bldg")
+    feeder_load = jnp.transpose(lax.psum(partial_load, "bldg"), (1, 0, 2))
     new_price = jnp.maximum(0.0, feeder_price + (feeder_load - feeder_limit[None, :, :]) / FEED)
     return (iterate, new_multiplier, new_price)
 

time: 487 us -> 180 us (0.37); the launches traced: 478 us -> 179 us
  matrix products: 291 us -> 4.07 us
  Pallas kernels: 0 us -> 55.8 us
  local copies, waits for them, and re-layouts: 82.7 us -> 39.3 us
  other arithmetic: 43.8 us -> 11.6 us
  waiting for transfers between devices: 0.34 us -> 8.49 us
    dot_general x14 -> x0, matrix products: 279 us -> none  [the longest x12 275 us: per_device(): primal = jnp.einsum('btk,sbk->sbt', inverse, right_side, precision=HIGHEST)]
    pallas_call x0 -> x1, Pallas kernels: none -> 55.8 us  [prox(): pl.pallas_call(prox_kernel, grid=(count // block,), in_specs=[big, whole2...]
    add x11 -> x0, other arithmetic: 37.1 us -> none  [per_device(): right_side = iterate - scaled_dual + fixed_part]
    dot_general x13 -> x0, local copies, waits for them, and re-layouts: 35.5 us -> none  [the longest x12 33.1 us: per_device(): primal = jnp.einsum('btk,sbk->sbt', inverse, right_side, precision=HIGHEST)]
    add x12 -> x0, local copies, waits for them, and re-layouts: 34.2 us -> none  [per_device(): right_side = iterate - scaled_dual + fixed_part]
    unnamed x25 -> x34, local copies, waits for them, and re-layouts: 12.3 us -> 30.7 us
    psum x1, waiting for transfers between devices: 0.32 us -> 8.48 us  [per_device(): lax.psum((sums_list[0], sums_list[1], sums_list[2], totals_list[0], total...]
    dot_general x3 -> x2, matrix products: 9.17 us -> 2.33 us  [section_sums(): jnp.einsum('ns,sbt->nbt', weighted, block, precision=HIGHEST)]
  transfers between devices with their start and end apart: 1 -> 1, of which waited for: 1 -> 1; matrix products, arithmetic and copies ran while one was open for 3% -> 2% of each run, Pallas kernels for 0% -> 0%
where the time goes in v1:
time: 180 us; the launch traced here: 179 us
  Pallas kernels  55.8 us (31%)
  blocking collectives  45.7 us (25%)
  local copies, waits for them, and re-layouts  39.3 us (22%)
  between operations  14.2 us (8%)
  other arithmetic  11.6 us (6%)
  waiting for transfers between devices  8.49 us (5%)
  matrix products  4.07 us (2%)
    pallas_call x1, Pallas kernels, prox(): pl.pallas_call(prox_kernel, grid=(count // block,), in_specs=[big, whole2...  55.8 us
    unnamed x34, local copies, waits for them, and re-layouts  30.7 us
    psum x1, blocking collectives, per_device(): lax.psum((sums_list[0], sums_list[1], sums_list[2], totals_list[0], total...  24.2 us
    psum x1, blocking collectives, per_device(): feeder_load = jnp.transpose(lax.psum(partial_load, 'bldg'), (1, 0, 2))  21.5 us
    psum x1, waiting for transfers between devices, per_device(): lax.psum((sums_list[0], sums_list[1], sums_list[2], totals_list[0], total...  8.48 us
    add x1, other arithmetic, per_device(): new_multiplier = multiplier + 0.5 * (iterate - mean)  5.88 us
    slice x2, local copies, waits for them, and re-layouts, section_sums(): block = shared_part[:, :, level * section_len:(level + 1) * section_len]  4.52 us
    dot_general x1, other arithmetic, section_sums(): jnp.einsum('ns,sbt->nbt', weighted, block, precision=HIGHEST)  4.27 us
  transfers between devices with their start and end apart: 1, of which 1 were waited for; matrix products, arithmetic and copies ran while one was open for 2% of the time, Pallas kernels for 0%

profile of v1, /device:TPU:0, one launch (start us, length us, event | category | flops | bytes accessed | tf_op | source)
XLA Modules:
  0.0 179.3 jit_solution(5020865577190835173)
XLA Ops:
  7.2 0.0 all-reduce.4.cloned.1.call-start
  7.2 2.8 %copy.15.mult_ref = f32[16,256,96]{2,1,0:T(8,128)} copy(f32[16,256,96]{1,2,0:T(8,128)} %param.14) | data formatting | bytes 3145728 | tf_op args[3]
  10.0 0.0 copy-start.7
  10.0 11.8 %copy.17.inv_ref = f32[256,96,96]{2,1,0:T(8,128)} copy(f32[256,96,96]{0,2,1:T(8,128)} %param.16) | data formatting | bytes 18874368 | tf_op args[5]
  21.8 0.0 copy-done.7
  21.8 1.8 %copy.14.demand_ref = f32[16,256,96]{2,1,0:T(8,128)} copy(f32[16,256,96]{1,2,0:T(8,128)S(1)} %copy-done.7) | data formatting | bytes 3145728 | tf_op args[0]
  23.6 0.0 copy-start.8
  23.6 0.0 copy-start.4
  23.6 0.0 copy-start.5
  23.6 0.0 copy-start.6
  23.6 2.9 %copy.16.prev_ref = f32[16,256,96]{2,1,0:T(8,128)} copy(f32[16,256,96]{1,2,0:T(8,128)} %param.15) | data formatting | bytes 3145728 | tf_op args[4]
  26.5 0.0 copy-done.8
  26.5 0.1 copy.18.limit_ref
  26.6 0.0 copy-done.4
  26.6 0.0 copy-done.5
  26.6 0.0 copy-done.6
  26.6 0.0 copy-start
  26.7 1.6 copy-done
  28.2 0.0 copy-start.2
  28.2 1.6 copy-done.2
  29.8 0.0 copy-start.3
  29.8 1.6 copy-done.3
  31.4 0.0 copy-start.9
  31.4 55.8 %prox.1 = (f32[16,256,96]{2,1,0:T(8,128)S(1)}, f32[8,16,96]{2,1,0:T(8,128)S(1)}) custom-call(f32[16,256,96]{2,1,0:T(8,128)S(1)} %copy-done.2, f32[16,96]{1,0:T(8,128)S(1)} %copy-done.5, f32[16,8,96]{2,1,0:T(8,128)S(1)} %copy-done.4, f32[16,256,96]{2,1,0:T(8,128)S(1)} %copy-done, f32[16,256,96]{2,1,0:T(8,128)S(1)} %copy-done.3, f32[256,96,96]{2,1,0:T(8,128)} %copy.17.inv_ref, ...), custom_call_target="tpu_custom_call" | custom-call | tf_op jit(solution)/shard_map/prox/pallas_call | solution.py:98
  87.3 0.0 copy-done.9
  87.3 4.3 %multiply_reduce_fusion = (f32[256,24]{1,0:T(8,128)S(1)}, f32[16,256,24]{2,1,0:T(8,128)}, f32[16,256,24]{2,1,0:T(8,128)}, f32[16,256,24]{2,1,0:T(8,128)}) fusion(f32[16,256,96]{2,1,0:T(8,128)S(1)} %get-tuple-element.7, f32[16]{0:T(128)S(1)} %copy-done.9), kind=kLoop, calls=%fused_computation.3 | loop fusion | flops 190464 | bytes 2777152 | tf_op jit(solution)/shard_map/ns,sbt->nbt/dot_general | solution.py:28
  91.6 0.0 copy-start.11
  91.6 2.3 %copy.30 = f32[16,256,24]{1,0,2:T(8,128)S(1)} copy(f32[16,256,24]{2,1,0:T(8,128)} %get-tuple-element.18) | data formatting | bytes 786432 | tf_op jit(solution)/shard_map/slice | solution.py:27
  93.8 0.0 copy-done.11
  93.8 0.0 copy-start.10
  93.9 2.3 %copy.29 = f32[16,256,24]{1,0,2:T(8,128)S(1)} copy(f32[16,256,24]{2,1,0:T(8,128)} %get-tuple-element.19) | data formatting | bytes 786432 | tf_op jit(solution)/shard_map/slice | solution.py:27
  96.1 1.3 fusion.9
  97.5 1.0 fusion.12
  98.5 0.0 all-reduce.4.cloned.1.call-update
  98.5 0.1 select_reduce_fusion
  98.6 0.6 reduce_sum.29
  99.2 21.5 %psum.55 = f32[8,16,96]{2,1,0:T(8,128)S(1)} all-reduce(f32[8,16,96]{2,1,0:T(8,128)S(1)} %get-tuple-element.6), channel_id=1, replica_groups=mesh['scen'=8,'bldg'=4] {'bldg'}, use_global_device_ids=true, to_apply=%region_9.0 | all-reduce | flops 12288 | bytes 98304 | tf_op jit(solution)/shard_map/psum | solution.py:153
  120.7 0.0 copy-done.10
  120.7 0.1 select_reduce_fusion.1
  120.9 24.2 %all-reduce = (f32[16]{0:T(128)S(1)}, f32[8]{0:T(128)S(1)}, f32[1,256,24]{2,1,0:T(8,128)S(1)}, f32[]{:T(128)}) all-reduce(f32[16]{0:T(128)S(1)} %select_reduce_fusion, f32[8]{0:T(128)S(1)} %select_reduce_fusion.1, f32[1,256,24]{2,1,0:T(8,128)S(1)} %bitcast.25, f32[]{:T(128)} %reduce_sum.29), channel_id=1, replica_groups=mesh['scen'=8,'bldg'=4] {'scen'}, use_global_device_ids=true, to_apply=%region_8.0 | all-reduce | flops 6169 | bytes 49352 | tf_op jit(solution)/shard_map/psum | solution.py:146
  145.0 1.7 copy.23
  146.7 0.7 copy.25
  147.4 0.6 divide_bitcast_fusion
  148.0 8.5 %all-reduce.4.cloned.1.call-done = (f32[16,256,24]{1,0,2:T(8,128)}, f32[8,256,24]{1,0,2:T(8,128)}) async-done(((f32[16,256,24]{1,0,2:T(8,128)}, f32[8,256,24]{1,0,2:T(8,128)}), (f32[16,256,24]{1,0,2:T(8,128)}, f32[8,256,24]{1,0,2:T(8,128)})) %all-reduce.4.cloned.1.call-update) | async-done | bytes 589840 | tf_op jit(solution)/shard_map/psum | solution.py:146
  156.5 0.0 copy-start.12
  156.5 1.4 fusion.5
  157.9 1.9 %copy.19 = f32[16,256,24]{2,1,0:T(8,128)} copy(f32[16,256,24]{1,0,2:T(8,128)S(1)} %fusion.5) | data formatting | bytes 786432 | tf_op jit(solution)/shard_map/ns,nbt->sbt/dot_general | solution.py:37
  159.8 0.0 copy-done.12
  159.8 0.4 fusion.2
  160.2 2.0 %copy.20 = f32[16,256,24]{2,1,0:T(8,128)} copy(f32[16,256,24]{1,0,2:T(8,128)S(1)} %fusion.2) | data formatting | bytes 786432 | tf_op jit(solution)/shard_map/ns,nbt->sbt/dot_general | solution.py:37
  162.2 0.0 copy-start.1
  162.2 0.2 dot_general.25
  162.4 1.4 copy-done.1
  163.8 5.9 %fusion.1 = f32[16,256,96]{2,1,0:T(8,128)} fusion(f32[16,256,96]{2,1,0:T(8,128)S(1)} %copy-done.1, f32[16,256,96]{2,1,0:T(8,128)S(1)} %get-tuple-element.7, f32[16,256,24]{2,1,0:T(8,128)} %get-tuple-element.17, f32[16,256,24]{2,1,0:T(8,128)} %copy.20, f32[16,256,24]{2,1,0:T(8,128)} %copy.19, f32[16,256,24]{2,1,0:T(8,128)S(1)} %dot_general.25), kind=kLoop, calls=%fused_computation.2 | loop fusion | flops 2359296 | bytes 6291456 | tf_op jit(solution)/shard_map/add | solution.py:152
  169.6 2.8 %copy.24 = f32[16,256,96]{1,2,0:T(8,128)} copy(f32[16,256,96]{2,1,0:T(8,128)} %fusion.1) | data formatting | bytes 3145728
  (2 shorter events, 0.0 us)
Async XLA Ops:
  7.2 149.3 %all-reduce.4.cloned.1.call-start = ((), (), s32[]{:S(2)}) async-start(), calls=%async_computation | async-start | bytes 1179648 | tf_op jit(solution)/shard_map/psum | solution.py:146
  10.0 11.8 %copy-start.7 = (f32[16,256,96]{1,2,0:T(8,128)S(1)}, f32[16,256,96]{1,2,0:T(8,128)}, u32[]{:S(2)}) copy-start(f32[16,256,96]{1,2,0:T(8,128)} %param.11) | copy-start | bytes 4718596
  23.6 2.9 %copy-start.8 = (f32[256,96]{0,1:T(8,128)S(1)}, f32[256,96]{0,1:T(8,128)}, u32[]{:S(2)}) copy-start(f32[256,96]{0,1:T(8,128)} %param.17) | copy-start | bytes 294916
  23.6 3.0 %copy-start.4 = (f32[16,8,96]{2,1,0:T(8,128)S(1)}, f32[16,8,96]{2,1,0:T(8,128)}, u32[]{:S(2)}) copy-start(f32[16,8,96]{2,1,0:T(8,128)} %price_ref.1) | copy-start | bytes 147460
  23.6 3.0 %copy-start.5 = (f32[16,96]{1,0:T(8,128)S(1)}, f32[16,96]{1,0:T(8,128)}, u32[]{:S(2)}) copy-start(f32[16,96]{1,0:T(8,128)} %tariff_ref.1) | copy-start | bytes 18436
  23.6 3.0 %copy-start.6 = (s32[256]{0:T(256)S(1)}, s32[256]{0:T(256)}, u32[]{:S(2)}) copy-start(s32[256]{0:T(256)} %feeder_ref.1) | copy-start | bytes 3076
  26.6 1.6 copy-start
  28.2 1.6 copy-start.2
  29.8 1.6 copy-start.3
  31.4 55.9 %copy-start.9 = (f32[16]{0:T(128)S(1)}, f32[16]{0:T(128)}, u32[]{:S(2)}) copy-start(f32[16]{0:T(128)} %param.18) | copy-start | bytes 196
  91.6 2.3 %copy-start.11 = (s32[2,16]{1,0:T(2,128)S(1)}, s32[2,16]{1,0:T(2,128)}, u32[]{:S(2)}) copy-start(s32[2,16]{1,0:T(2,128)} %param.19) | copy-start | bytes 388
  93.8 26.8 %copy-start.10 = (f32[8,96]{1,0:T(8,128)S(1)}, f32[8,96]{1,0:T(8,128)}, u32[]{:S(2)}) copy-start(f32[8,96]{1,0:T(8,128)} %param.21) | copy-start | bytes 9220
  156.5 3.3 %copy-start.12 = (f32[16,256,24]{1,0,2:T(8,128)S(1)}, f32[16,256,24]{1,0,2:T(8,128)}, u32[]{:S(2)}) copy-start(f32[16,256,24]{1,0,2:T(8,128)} %get-tuple-element.14) | copy-start | bytes 1179652
  162.2 1.6 copy-start.1
Sparse Core Ops, SparseCore 0:
  98.6 57.8 all-reduce.3

commit v2 on v1

--- a/solution.py
+++ b/solution.py
@@ -1,3 +1,5 @@
+import functools
+
 import jax
 import jax.numpy as jnp
 from jax import lax
@@ -7,35 +9,6 @@
 
 FEED = 128
 PROX = 12
-
-
-HIGHEST = lax.Precision.HIGHEST
-
-
-def node_tables(nodes, fine_count):
-    root = jnp.ones((1, nodes.shape[1]), jnp.float32)
-    coarse = (nodes[0][None, :] == jnp.arange(8)[:, None]).astype(jnp.float32)
-    fine_table = (nodes[1][None, :] == jnp.arange(fine_count)[:, None]).astype(jnp.float32)
-    return [root, coarse, fine_table]
-
-
-def section_sums(tables, scen_weight, shared_part, section_len):
-    sums_list = []
-    totals_list = []
-    for level in range(3):
-        weighted = tables[level] * scen_weight[None, :]
-        block = shared_part[:, :, level * section_len : (level + 1) * section_len]
-        sums_list.append(jnp.einsum("ns,sbt->nbt", weighted, block, precision=HIGHEST))
-        totals_list.append(jnp.sum(weighted, axis=1))
-    return (sums_list, totals_list)
-
-
-def spread_means(tables, sums_list, totals_list):
-    pieces = []
-    for level in range(3):
-        means = sums_list[level] / totals_list[level][:, None, None]
-        pieces.append(jnp.einsum("ns,nbt->sbt", tables[level], means, precision=HIGHEST))
-    return jnp.concatenate(pieces, axis=2)
 
 
 BLOCK = 16
@@ -119,6 +92,174 @@
         compiler_params=pltpu.CompilerParams(dimension_semantics=("arbitrary",), vmem_limit_bytes=40 * 2**20),
         name="prox",
     )(demand, tariff, feeder_price, multiplier, previous_mean, inverse, power_limit, building_feeder)
+
+
+COARSE = 8
+
+
+def sums_kernel(weighted_ref, plan_ref, out_ref):
+    nodes, scen = weighted_ref.shape
+    lanes = plan_ref.shape[2]
+    length = plan_ref.shape[1] // 4
+    tail = nodes * length
+    out_ref[pl.ds(tail, out_ref.shape[0] - tail), :] = jnp.zeros((out_ref.shape[0] - tail, lanes), jnp.float32)
+
+    def add_node(level):
+        def body(n, carry):
+            factor = weighted_ref[n, 0]
+            total = factor
+            acc = factor * plan_ref[0, level * length : (level + 1) * length, :]
+            for s in range(1, scen):
+                factor = weighted_ref[n, s]
+                total = total + factor
+                acc = acc + factor * plan_ref[s, level * length : (level + 1) * length, :]
+            out_ref[pl.ds(pl.multiple_of(n * length, 8), length), :] = acc
+            out_ref[pl.ds(tail + n, 1), :] = jnp.full((1, lanes), total, jnp.float32)
+            return carry
+
+        return body
+
+    for level, (low, high) in enumerate(((0, 1), (1, 1 + COARSE), (1 + COARSE, nodes))):
+        lax.fori_loop(low, high, add_node(level), 0)
+
+
+def node_sums(weighted, plan_t, length, devices):
+    nodes = weighted.shape[0]
+    unit = 8 * devices
+    rows = (nodes * length + nodes + unit - 1) // unit * unit
+    return pl.pallas_call(
+        sums_kernel,
+        in_specs=[pl.BlockSpec(memory_space=pltpu.SMEM), pl.BlockSpec(memory_space=pltpu.VMEM)],
+        out_specs=pl.BlockSpec(memory_space=pltpu.VMEM),
+        out_shape=jax.ShapeDtypeStruct((rows, plan_t.shape[2]), jnp.float32),
+        compiler_params=pltpu.CompilerParams(vmem_limit_bytes=24 * 2**20),
+        name="node_sums",
+    )(weighted, plan_t)
+
+
+def exchange_kernel(
+    scen_size, bldg_size, sums_ref, load_ref, full_ref, total_ref,
+    landed, own, load_landed, all_rows, rs_send, rs_recv, ag_send, ag_recv, load_send, load_recv,
+):
+    me, column = lax.axis_index("scen"), lax.axis_index("bldg")
+    chunk = own.shape[0]
+    peers = [(lax.rem(me + k, scen_size), column) for k in range(1, scen_size)]
+    beside = [(me, lax.rem(column + k, bldg_size)) for k in range(1, bldg_size)]
+    barrier = pltpu.get_barrier_semaphore()
+    for peer in peers + beside:
+        pl.semaphore_signal(barrier, inc=1, device_id=peer, device_id_type=pl.DeviceIdType.MESH)
+    pl.semaphore_wait(barrier, scen_size + bldg_size - 2)
+
+    def rows_of(index):
+        return pl.ds(pl.multiple_of(index * chunk, 8), chunk)
+
+    scatter = []
+    for k, peer in enumerate(peers):
+        copy = pltpu.make_async_remote_copy(
+            src_ref=sums_ref.at[rows_of(peer[0])], dst_ref=landed.at[k],
+            send_sem=rs_send.at[k], recv_sem=rs_recv.at[k],
+            device_id=peer, device_id_type=pl.DeviceIdType.MESH,
+        )
+        copy.start()
+        scatter.append(copy)
+    loads = []
+    for k, peer in enumerate(beside):
+        copy = pltpu.make_async_remote_copy(
+            src_ref=load_ref, dst_ref=load_landed.at[k],
+            send_sem=load_send.at[k], recv_sem=load_recv.at[k],
+            device_id=peer, device_id_type=pl.DeviceIdType.MESH,
+        )
+        copy.start()
+        loads.append(copy)
+    for copy in scatter:
+        copy.wait_recv()
+    acc = sums_ref[rows_of(me), :]
+    for k in range(scen_size - 1):
+        acc = acc + landed[k]
+    own[...] = acc
+    all_rows[rows_of(me), :] = acc
+    gather = []
+    for k, peer in enumerate(peers):
+        copy = pltpu.make_async_remote_copy(
+            src_ref=own, dst_ref=all_rows.at[rows_of(me)],
+            send_sem=ag_send.at[k], recv_sem=ag_recv.at[k],
+            device_id=peer, device_id_type=pl.DeviceIdType.MESH,
+        )
+        copy.start()
+        gather.append(copy)
+    for copy in loads:
+        copy.wait_recv()
+    total = load_ref[...]
+    for k in range(bldg_size - 1):
+        total = total + load_landed[k]
+    total_ref[...] = total
+    for copy in gather:
+        copy.wait_recv()
+    full_ref[...] = all_rows[...]
+    for copy in scatter + loads + gather:
+        copy.wait_send()
+
+
+def exchange(local, load):
+    scen_size, bldg_size = lax.axis_size("scen"), lax.axis_size("bldg")
+    rows, lanes = local.shape
+    chunk = rows // scen_size
+    dma = pltpu.SemaphoreType.DMA
+    vmem = pl.BlockSpec(memory_space=pltpu.VMEM)
+    return pl.pallas_call(
+        functools.partial(exchange_kernel, scen_size, bldg_size),
+        in_specs=[vmem, vmem],
+        out_specs=[vmem, vmem],
+        out_shape=[
+            jax.ShapeDtypeStruct((rows, lanes), jnp.float32),
+            jax.ShapeDtypeStruct(load.shape, jnp.float32),
+        ],
+        scratch_shapes=[
+            pltpu.VMEM((scen_size - 1, chunk, lanes), jnp.float32),
+            pltpu.VMEM((chunk, lanes), jnp.float32),
+            pltpu.VMEM((bldg_size - 1,) + load.shape, jnp.float32),
+            pltpu.VMEM((rows, lanes), jnp.float32),
+            dma((scen_size - 1,)), dma((scen_size - 1,)),
+            dma((scen_size - 1,)), dma((scen_size - 1,)),
+            dma((bldg_size - 1,)), dma((bldg_size - 1,)),
+        ],
+        compiler_params=pltpu.CompilerParams(
+            collective_id=0, has_side_effects=True, vmem_limit_bytes=24 * 2**20
+        ),
+        name="exchange",
+    )(local, load)
+
+
+def spread_kernel(nodes, places_ref, full_ref, plan_ref, mult_ref, out_ref, mean_ref):
+    scen, slots, _ = plan_ref.shape
+    length = slots // 4
+    tail = nodes * length
+
+    def divide(n, carry):
+        share = full_ref[pl.ds(pl.multiple_of(n * length, 8), length), :]
+        mean_ref[n] = share / full_ref[pl.ds(tail + n, 1), :]
+        return carry
+
+    lax.fori_loop(0, nodes, divide, 0)
+    for s in range(scen):
+        for level in range(4):
+            part = slice(level * length, (level + 1) * length)
+            plan = plan_ref[s, part, :]
+            mean = plan if level == 3 else mean_ref[places_ref[level, s]]
+            out_ref[s, part, :] = mult_ref[s, part, :] + 0.5 * (plan - mean)
+
+
+def spread(places, full, plan_t, mult_t, nodes):
+    vmem = pl.BlockSpec(memory_space=pltpu.VMEM)
+    return pl.pallas_call(
+        functools.partial(spread_kernel, nodes),
+        in_specs=[pl.BlockSpec(memory_space=pltpu.SMEM), vmem, vmem, vmem],
+        out_specs=vmem,
+        out_shape=jax.ShapeDtypeStruct(plan_t.shape, jnp.float32),
+        scratch_shapes=[pltpu.VMEM((nodes, plan_t.shape[1] // 4, plan_t.shape[2]), jnp.float32)],
+        compiler_params=pltpu.CompilerParams(vmem_limit_bytes=24 * 2**20),
+        name="spread",
+    )(places, full, plan_t, mult_t)
 
 
 def per_device(
@@ -139,18 +280,19 @@
     iterate, partial_load = prox(
         demand, tariff, feeder_price, multiplier, previous_mean, inverse, power_limit, building_feeder
     )
-    shared_part = iterate[:, :, : 3 * section_len]
-    fine_count = lax.axis_size("scen") * demand.shape[0] // 8
-    tables = node_tables(tree_node, fine_count)
-    sums_list, totals_list = section_sums(tables, weights, shared_part, section_len)
-    summed = lax.psum(
-        (sums_list[0], sums_list[1], sums_list[2], totals_list[0], totals_list[1], totals_list[2]),
-        "scen",
-    )
-    early_mean = spread_means(tables, list(summed[:3]), list(summed[3:]))
-    mean = jnp.concatenate([early_mean, iterate[:, :, 3 * section_len :]], axis=2)
-    new_multiplier = multiplier + 0.5 * (iterate - mean)
-    feeder_load = jnp.transpose(lax.psum(partial_load, "bldg"), (1, 0, 2))
+    plan_t = jnp.transpose(iterate, (0, 2, 1))
+    mult_t = jnp.transpose(multiplier, (0, 2, 1))
+    devices = lax.axis_size("scen")
+    fine_count = devices * demand.shape[0] // 8
+    offsets = jnp.array([[1], [1 + COARSE]], jnp.int32)
+    places = jnp.concatenate([jnp.zeros_like(tree_node[:1]), tree_node + offsets], axis=0)
+    nodes = 1 + COARSE + fine_count
+    hits = places[:, None, :] == jnp.arange(nodes)[None, :, None]
+    weighted = jnp.sum(hits.astype(jnp.float32), axis=0) * weights[None, :]
+    local = node_sums(weighted, plan_t, section_len, devices)
+    full, feeder_load = exchange(local, partial_load)
+    new_multiplier = jnp.transpose(spread(places, full, plan_t, mult_t, nodes), (0, 2, 1))
+    feeder_load = jnp.transpose(feeder_load, (1, 0, 2))
     new_price = jnp.maximum(0.0, feeder_price + (feeder_load - feeder_limit[None, :, :]) / FEED)
     return (iterate, new_multiplier, new_price)
 

time: 180 us -> 111 us (0.62)
  blocking collectives: 45.7 us -> 0 us
  Pallas kernels: 55.8 us -> 81.9 us
  between operations: 14.2 us -> 0.78 us
  local copies, waits for them, and re-layouts: 39.3 us -> 26.4 us
  other arithmetic: 11.6 us -> 0.17 us
  waiting for transfers between devices: 8.49 us -> 0 us
  matrix products: 4.07 us -> 0 us
    psum x2 -> x0, blocking collectives: 45.7 us -> none  [the longest x1 24.2 us: per_device(): lax.psum((sums_list[0], sums_list[1], sums_list[2], totals_list[0], total...]
    pallas_call x0 -> x3, Pallas kernels: none -> 26.1 us  [the longest x1 22 us: exchange(): pl.pallas_call(functools.partial(exchange_kernel, scen_size, bldg_size),...]
    psum x1 -> x0, waiting for transfers between devices: 8.48 us -> none  [per_device(): lax.psum((sums_list[0], sums_list[1], sums_list[2], totals_list[0], total...]
    add x1, other arithmetic: 5.88 us -> 0.07 us  [per_device(): tree_node + offsets]
    dot_general x2 -> x0, other arithmetic: 4.91 us -> none  [the longest x1 4.27 us: section_sums(): jnp.einsum('ns,sbt->nbt', weighted, block, precision=HIGHEST)]
    slice x2 -> x0, local copies, waits for them, and re-layouts: 4.52 us -> none  [section_sums(): block = shared_part[:, :, level * section_len:(level + 1) * section_len]]
    unnamed x34 -> x33, local copies, waits for them, and re-layouts: 30.7 us -> 26.3 us
    dot_general x3 -> x0, local copies, waits for them, and re-layouts: 4.09 us -> none  [spread_means(): jnp.einsum('ns,nbt->sbt', tables[level], means, precision=HIGHEST)]
  transfers between devices with their start and end apart: 1 -> 0, of which waited for: 1 -> 0; matrix products, arithmetic and copies ran while one was open for 2% -> 0% of each run, Pallas kernels for 0% -> 0%
where the time goes in v2:
time: 111 us; the launch traced here: 109 us
  Pallas kernels  81.9 us (74%)
  local copies, waits for them, and re-layouts  26.4 us (24%)
    pallas_call x1, Pallas kernels, prox(): pl.pallas_call(prox_kernel, grid=(count // block,), in_specs=[big, whole2...  55.9 us
    unnamed x33, local copies, waits for them, and re-layouts  26.3 us
    pallas_call x1, Pallas kernels, exchange(): pl.pallas_call(functools.partial(exchange_kernel, scen_size, bldg_size),...  22 us
    pallas_call x1, Pallas kernels, spread(): pl.pallas_call(functools.partial(spread_kernel, nodes), in_specs=[pl.Bloc...  2.28 us

profile of v2, /device:TPU:0, one launch (start us, length us, event | category | flops | bytes accessed | tf_op | source)
XLA Modules:
  0.0 109.3 jit_solution(6225056734262686416)
XLA Ops:
  0.6 11.6 %copy.37.inv_ref = f32[256,96,96]{2,1,0:T(8,128)} copy(f32[256,96,96]{0,2,1:T(8,128)} %param.17) | data formatting | bytes 18874368 | tf_op args[5]
  12.2 1.8 %copy.34.demand_ref = f32[16,256,96]{2,1,0:T(8,128)S(1)} copy(f32[16,256,96]{1,2,0:T(8,128)} %param.12) | data formatting | bytes 3145728 | tf_op args[0]
  14.1 2.8 %copy.35.mult_ref = f32[16,256,96]{2,1,0:T(8,128)} copy(f32[16,256,96]{1,2,0:T(8,128)} %param.15) | data formatting | bytes 3145728 | tf_op args[3]
  16.9 0.0 copy-start.8
  16.9 0.0 copy-start.5
  16.9 0.0 copy-start.6
  16.9 0.0 copy-start.7
  16.9 2.8 %copy.36.prev_ref = f32[16,256,96]{2,1,0:T(8,128)} copy(f32[16,256,96]{1,2,0:T(8,128)} %param.16) | data formatting | bytes 3145728 | tf_op args[4]
  19.7 0.0 copy-done.8
  19.7 0.1 copy.38.limit_ref
  19.8 0.0 copy-done.5
  19.8 0.0 copy-done.6
  19.8 0.0 copy-done.7
  19.8 0.0 copy-start.1
  19.8 1.6 %copy-done.1 = f32[16,256,96]{2,1,0:T(8,128)S(1)} copy-done((f32[16,256,96]{2,1,0:T(8,128)S(1)}, f32[16,256,96]{2,1,0:T(8,128)}, u32[]{:S(2)}) %copy-start.1) | copy-done | bytes 1572888
  21.4 0.0 copy-start.2
  21.4 1.6 %copy-done.2 = f32[16,256,96]{2,1,0:T(8,128)S(1)} copy-done((f32[16,256,96]{2,1,0:T(8,128)S(1)}, f32[16,256,96]{2,1,0:T(8,128)}, u32[]{:S(2)}) %copy-start.2) | copy-done | bytes 1572888
  23.0 55.9 %prox.1 = (f32[16,256,96]{2,1,0:T(8,128)S(1)}, f32[8,16,96]{2,1,0:T(8,128)S(1)}) custom-call(f32[16,256,96]{2,1,0:T(8,128)S(1)} %copy.34.demand_ref, f32[16,96]{1,0:T(8,128)S(1)} %copy-done.6, f32[16,8,96]{2,1,0:T(8,128)S(1)} %copy-done.5, f32[16,256,96]{2,1,0:T(8,128)S(1)} %copy-done.1, f32[16,256,96]{2,1,0:T(8,128)S(1)} %copy-done.2, ...), custom_call_target="tpu_custom_call" | custom-call | tf_op jit(solution)/shard_map/prox/pallas_call | solution.py:71
  78.9 0.0 copy-start.4
  78.9 1.3 %copy-done.4 = f32[16,256,96]{2,1,0:T(8,128)} copy-done((f32[16,256,96]{2,1,0:T(8,128)}, f32[16,256,96]{2,1,0:T(8,128)S(1)}, u32[]{:S(2)}) %copy-start.4) | copy-done | bytes 1572888
  80.2 0.0 copy-start.10
  80.3 0.0 copy-start.12
  80.3 0.0 copy-start.11
  80.3 1.9 %copy.43 = f32[16,256,96]{1,2,0:T(8,128)S(1)} copy(f32[16,256,96]{2,1,0:T(8,128)} %copy-done.4) | data formatting | bytes 3145728
  82.2 0.0 copy-start
  82.2 0.0 copy-start.3
  82.2 0.0 copy-done.10
  82.2 0.0 copy-done.12
  82.2 0.1 broadcast_add_fusion
  82.3 0.1 convert_reduce_fusion
  82.4 0.1 copy.39
  82.5 0.0 copy-done.11
  82.5 1.8 %node_sums.1.sums_ref = f32[640,256]{1,0:T(8,128)S(1)} custom-call(f32[25,16]{1,0:T(8,128)S(1)} %broadcast_multiply_fusion.weighted_ref, f32[16,96,256]{2,1,0:T(8,128)S(1)} %bitcast.7), custom_call_target="tpu_custom_call" | custom-call | tf_op jit(solution)/shard_map/node_sums/pallas_call | solution.py:130
  84.3 22.0 %exchange.1 = (f32[640,256]{1,0:T(8,128)S(1)}, f32[8,16,96]{2,1,0:T(8,128)S(1)}) custom-call(f32[640,256]{1,0:T(8,128)S(1)} %node_sums.1.sums_ref, f32[8,16,96]{2,1,0:T(8,128)S(1)} %get-tuple-element.8.load_ref), custom_call_target="tpu_custom_call" | custom-call | tf_op jit(solution)/shard_map/exchange/pallas_call | solution.py:209
  106.3 0.0 copy-done.3
  106.3 0.0 copy-start.9
  106.3 2.3 %spread.1 = f32[16,96,256]{2,1,0:T(8,128)} custom-call(s32[3,16]{1,0:T(4,128)S(1)} %concatenate.3.places_ref, f32[640,256]{1,0:T(8,128)S(1)} %get-tuple-element.9.full_ref, f32[16,96,256]{2,1,0:T(8,128)S(1)} %bitcast.8, f32[16,96,256]{2,1,0:T(8,128)S(1)} %bitcast.9), custom_call_target="tpu_custom_call" | custom-call | tf_op jit(solution)/shard_map/spread/pallas_call | solution.py:254
  108.6 0.0 copy-done
  108.6 0.0 copy-done.9
  108.6 0.7 copy.44
  (3 shorter events, 0.0 us)
Async XLA Ops:
  16.9 2.9 %copy-start.8 = (f32[256,96]{0,1:T(8,128)S(1)}, f32[256,96]{0,1:T(8,128)}, u32[]{:S(2)}) copy-start(f32[256,96]{0,1:T(8,128)} %param.18) | copy-start | bytes 294916
  16.9 3.0 %copy-start.5 = (f32[16,8,96]{2,1,0:T(8,128)S(1)}, f32[16,8,96]{2,1,0:T(8,128)}, u32[]{:S(2)}) copy-start(f32[16,8,96]{2,1,0:T(8,128)} %price_ref.1) | copy-start | bytes 147460
  16.9 3.0 %copy-start.6 = (f32[16,96]{1,0:T(8,128)S(1)}, f32[16,96]{1,0:T(8,128)}, u32[]{:S(2)}) copy-start(f32[16,96]{1,0:T(8,128)} %tariff_ref.1) | copy-start | bytes 18436
  16.9 3.0 %copy-start.7 = (s32[256]{0:T(256)S(1)}, s32[256]{0:T(256)}, u32[]{:S(2)}) copy-start(s32[256]{0:T(256)} %feeder_ref.1) | copy-start | bytes 3076
  19.8 1.6 %copy-start.1 = (f32[16,256,96]{2,1,0:T(8,128)S(1)}, f32[16,256,96]{2,1,0:T(8,128)}, u32[]{:S(2)}) copy-start(f32[16,256,96]{2,1,0:T(8,128)} %copy.35.mult_ref) | copy-start | bytes 4718596
  21.4 1.6 %copy-start.2 = (f32[16,256,96]{2,1,0:T(8,128)S(1)}, f32[16,256,96]{2,1,0:T(8,128)}, u32[]{:S(2)}) copy-start(f32[16,256,96]{2,1,0:T(8,128)} %copy.36.prev_ref) | copy-start | bytes 4718596
  78.9 1.3 %copy-start.4 = (f32[16,256,96]{2,1,0:T(8,128)}, f32[16,256,96]{2,1,0:T(8,128)S(1)}, u32[]{:S(2)}) copy-start(f32[16,256,96]{2,1,0:T(8,128)S(1)} %get-tuple-element.17) | copy-start | bytes 4718596
  80.2 2.0 %copy-start.10 = (s32[2,16]{1,0:T(2,128)S(1)}, s32[2,16]{1,0:T(2,128)}, u32[]{:S(2)}) copy-start(s32[2,16]{1,0:T(2,128)} %param.20) | copy-start | bytes 388
  80.3 2.0 %copy-start.12 = (s32[2]{0:T(128)S(1)}, s32[2]{0:T(128)}, u32[]{:S(2)}) copy-start(s32[2]{0:T(128)} %constant.13) | copy-start | bytes 28
  80.3 2.2 %copy-start.11 = (f32[16]{0:T(128)S(1)}, f32[16]{0:T(128)}, u32[]{:S(2)}) copy-start(f32[16]{0:T(128)} %param.19) | copy-start | bytes 196
  82.2 26.4 %copy-start = (f32[16,256,96]{1,2,0:T(8,128)}, f32[16,256,96]{1,2,0:T(8,128)S(1)}, u32[]{:S(2)}) copy-start(f32[16,256,96]{1,2,0:T(8,128)S(1)} %copy.43) | copy-start | bytes 4718596
  82.2 24.1 %copy-start.3 = (f32[16,256,96]{1,2,0:T(8,128)S(1)}, f32[16,256,96]{1,2,0:T(8,128)}, u32[]{:S(2)}) copy-start(f32[16,256,96]{1,2,0:T(8,128)} %param.15) | copy-start | bytes 4718596
  106.3 2.3 %copy-start.9 = (f32[8,96]{1,0:T(8,128)S(1)}, f32[8,96]{1,0:T(8,128)}, u32[]{:S(2)}) copy-start(f32[8,96]{1,0:T(8,128)} %param.22) | copy-start | bytes 9220

commit v3 on v2

--- a/solution.py
+++ b/solution.py
@@ -11,7 +11,7 @@
 PROX = 12
 
 
-BLOCK = 16
+BLOCK = 64
 LANES = 128
 
 

time: 111 us -> 90 us (0.81)
  Pallas kernels: 81.9 us -> 61 us
    pallas_call x1, Pallas kernels: 55.9 us -> 35 us  [prox(): pl.pallas_call(prox_kernel, grid=(count // block,), in_specs=[big, whole2...]
where the time goes in v3:
time: 90 us; the launch traced here: 88.4 us
  Pallas kernels  61 us (68%)
  local copies, waits for them, and re-layouts  26.4 us (29%)
    pallas_call x1, Pallas kernels, prox(): pl.pallas_call(prox_kernel, grid=(count // block,), in_specs=[big, whole2...  35 us
    unnamed x33, local copies, waits for them, and re-layouts  26.3 us
    pallas_call x1, Pallas kernels, exchange(): pl.pallas_call(functools.partial(exchange_kernel, scen_size, bldg_size),...  22 us
    pallas_call x1, Pallas kernels, spread(): pl.pallas_call(functools.partial(spread_kernel, nodes), in_specs=[pl.Bloc...  2.28 us

profile of v3, /device:TPU:0, one launch (start us, length us, event | category | flops | bytes accessed | tf_op | source)
XLA Modules:
  0.0 88.4 jit_solution(10433568436858692122)
XLA Ops:
  0.6 11.6 %copy.37.inv_ref = f32[256,96,96]{2,1,0:T(8,128)} copy(f32[256,96,96]{0,2,1:T(8,128)} %param.17) | data formatting | bytes 18874368 | tf_op args[5]
  12.2 1.8 %copy.34.demand_ref = f32[16,256,96]{2,1,0:T(8,128)S(1)} copy(f32[16,256,96]{1,2,0:T(8,128)} %param.12) | data formatting | bytes 3145728 | tf_op args[0]
  14.1 2.8 %copy.35.mult_ref = f32[16,256,96]{2,1,0:T(8,128)} copy(f32[16,256,96]{1,2,0:T(8,128)} %param.15) | data formatting | bytes 3145728 | tf_op args[3]
  16.9 0.0 copy-start.8
  16.9 0.0 copy-start.5
  16.9 0.0 copy-start.6
  16.9 0.0 copy-start.7
  16.9 2.8 %copy.36.prev_ref = f32[16,256,96]{2,1,0:T(8,128)} copy(f32[16,256,96]{1,2,0:T(8,128)} %param.16) | data formatting | bytes 3145728 | tf_op args[4]
  19.7 0.0 copy-done.8
  19.7 0.1 copy.38.limit_ref
  19.8 0.0 copy-done.5
  19.8 0.0 copy-done.6
  19.8 0.0 copy-done.7
  19.8 0.0 copy-start.1
  19.8 1.6 %copy-done.1 = f32[16,256,96]{2,1,0:T(8,128)S(1)} copy-done((f32[16,256,96]{2,1,0:T(8,128)S(1)}, f32[16,256,96]{2,1,0:T(8,128)}, u32[]{:S(2)}) %copy-start.1) | copy-done | bytes 1572888
  21.4 0.0 copy-start.2
  21.4 1.6 %copy-done.2 = f32[16,256,96]{2,1,0:T(8,128)S(1)} copy-done((f32[16,256,96]{2,1,0:T(8,128)S(1)}, f32[16,256,96]{2,1,0:T(8,128)}, u32[]{:S(2)}) %copy-start.2) | copy-done | bytes 1572888
  23.0 35.0 %prox.1 = (f32[16,256,96]{2,1,0:T(8,128)S(1)}, f32[8,16,96]{2,1,0:T(8,128)S(1)}) custom-call(f32[16,256,96]{2,1,0:T(8,128)S(1)} %copy.34.demand_ref, f32[16,96]{1,0:T(8,128)S(1)} %copy-done.6, f32[16,8,96]{2,1,0:T(8,128)S(1)} %copy-done.5, f32[16,256,96]{2,1,0:T(8,128)S(1)} %copy-done.1, f32[16,256,96]{2,1,0:T(8,128)S(1)} %copy-done.2, ...), custom_call_target="tpu_custom_call" | custom-call | tf_op jit(solution)/shard_map/prox/pallas_call | solution.py:71
  58.0 0.0 copy-start.4
  58.0 1.3 %copy-done.4 = f32[16,256,96]{2,1,0:T(8,128)} copy-done((f32[16,256,96]{2,1,0:T(8,128)}, f32[16,256,96]{2,1,0:T(8,128)S(1)}, u32[]{:S(2)}) %copy-start.4) | copy-done | bytes 1572888
  59.3 0.0 copy-start.10
  59.3 0.0 copy-start.12
  59.3 0.0 copy-start.11
  59.3 1.9 %copy.43 = f32[16,256,96]{1,2,0:T(8,128)S(1)} copy(f32[16,256,96]{2,1,0:T(8,128)} %copy-done.4) | data formatting | bytes 3145728
  61.3 0.0 copy-start
  61.3 0.0 copy-start.3
  61.3 0.0 copy-done.10
  61.3 0.0 copy-done.12
  61.3 0.1 broadcast_add_fusion
  61.4 0.1 convert_reduce_fusion
  61.5 0.1 copy.39
  61.6 0.0 copy-done.11
  61.6 1.8 %node_sums.1.sums_ref = f32[640,256]{1,0:T(8,128)S(1)} custom-call(f32[25,16]{1,0:T(8,128)S(1)} %broadcast_multiply_fusion.weighted_ref, f32[16,96,256]{2,1,0:T(8,128)S(1)} %bitcast.7), custom_call_target="tpu_custom_call" | custom-call | tf_op jit(solution)/shard_map/node_sums/pallas_call | solution.py:130
  63.4 22.0 %exchange.1 = (f32[640,256]{1,0:T(8,128)S(1)}, f32[8,16,96]{2,1,0:T(8,128)S(1)}) custom-call(f32[640,256]{1,0:T(8,128)S(1)} %node_sums.1.sums_ref, f32[8,16,96]{2,1,0:T(8,128)S(1)} %get-tuple-element.8.load_ref), custom_call_target="tpu_custom_call" | custom-call | tf_op jit(solution)/shard_map/exchange/pallas_call | solution.py:209
  85.4 0.0 copy-done.3
  85.4 0.0 copy-start.9
  85.4 2.3 %spread.1 = f32[16,96,256]{2,1,0:T(8,128)} custom-call(s32[3,16]{1,0:T(4,128)S(1)} %concatenate.3.places_ref, f32[640,256]{1,0:T(8,128)S(1)} %get-tuple-element.9.full_ref, f32[16,96,256]{2,1,0:T(8,128)S(1)} %bitcast.8, f32[16,96,256]{2,1,0:T(8,128)S(1)} %bitcast.9), custom_call_target="tpu_custom_call" | custom-call | tf_op jit(solution)/shard_map/spread/pallas_call | solution.py:254
  87.7 0.0 copy-done
  87.7 0.0 copy-done.9
  87.7 0.7 copy.44
  (3 shorter events, 0.0 us)
Async XLA Ops:
  16.9 2.9 %copy-start.8 = (f32[256,96]{0,1:T(8,128)S(1)}, f32[256,96]{0,1:T(8,128)}, u32[]{:S(2)}) copy-start(f32[256,96]{0,1:T(8,128)} %param.18) | copy-start | bytes 294916
  16.9 3.0 %copy-start.5 = (f32[16,8,96]{2,1,0:T(8,128)S(1)}, f32[16,8,96]{2,1,0:T(8,128)}, u32[]{:S(2)}) copy-start(f32[16,8,96]{2,1,0:T(8,128)} %price_ref.1) | copy-start | bytes 147460
  16.9 3.0 %copy-start.6 = (f32[16,96]{1,0:T(8,128)S(1)}, f32[16,96]{1,0:T(8,128)}, u32[]{:S(2)}) copy-start(f32[16,96]{1,0:T(8,128)} %tariff_ref.1) | copy-start | bytes 18436
  16.9 3.0 %copy-start.7 = (s32[256]{0:T(256)S(1)}, s32[256]{0:T(256)}, u32[]{:S(2)}) copy-start(s32[256]{0:T(256)} %feeder_ref.1) | copy-start | bytes 3076
  19.8 1.6 %copy-start.1 = (f32[16,256,96]{2,1,0:T(8,128)S(1)}, f32[16,256,96]{2,1,0:T(8,128)}, u32[]{:S(2)}) copy-start(f32[16,256,96]{2,1,0:T(8,128)} %copy.35.mult_ref) | copy-start | bytes 4718596
  21.4 1.6 %copy-start.2 = (f32[16,256,96]{2,1,0:T(8,128)S(1)}, f32[16,256,96]{2,1,0:T(8,128)}, u32[]{:S(2)}) copy-start(f32[16,256,96]{2,1,0:T(8,128)} %copy.36.prev_ref) | copy-start | bytes 4718596
  58.0 1.3 %copy-start.4 = (f32[16,256,96]{2,1,0:T(8,128)}, f32[16,256,96]{2,1,0:T(8,128)S(1)}, u32[]{:S(2)}) copy-start(f32[16,256,96]{2,1,0:T(8,128)S(1)} %get-tuple-element.17) | copy-start | bytes 4718596
  59.3 2.0 %copy-start.10 = (s32[2,16]{1,0:T(2,128)S(1)}, s32[2,16]{1,0:T(2,128)}, u32[]{:S(2)}) copy-start(s32[2,16]{1,0:T(2,128)} %param.20) | copy-start | bytes 388
  59.3 2.0 %copy-start.12 = (s32[2]{0:T(128)S(1)}, s32[2]{0:T(128)}, u32[]{:S(2)}) copy-start(s32[2]{0:T(128)} %constant.13) | copy-start | bytes 28
  59.3 2.2 %copy-start.11 = (f32[16]{0:T(128)S(1)}, f32[16]{0:T(128)}, u32[]{:S(2)}) copy-start(f32[16]{0:T(128)} %param.19) | copy-start | bytes 196
  61.3 26.4 %copy-start = (f32[16,256,96]{1,2,0:T(8,128)}, f32[16,256,96]{1,2,0:T(8,128)S(1)}, u32[]{:S(2)}) copy-start(f32[16,256,96]{1,2,0:T(8,128)S(1)} %copy.43) | copy-start | bytes 4718596
  61.3 24.1 %copy-start.3 = (f32[16,256,96]{1,2,0:T(8,128)S(1)}, f32[16,256,96]{1,2,0:T(8,128)}, u32[]{:S(2)}) copy-start(f32[16,256,96]{1,2,0:T(8,128)} %param.15) | copy-start | bytes 4718596
  85.4 2.3 %copy-start.9 = (f32[8,96]{1,0:T(8,128)S(1)}, f32[8,96]{1,0:T(8,128)}, u32[]{:S(2)}) copy-start(f32[8,96]{1,0:T(8,128)} %param.22) | copy-start | bytes 9220
